TPU v7x, 32 devices: a whole 2x2x4 slice. The times are simulated.
32 devices in a mesh: parts: 2 (over y), tm: 4 (over z), axial: 2 (over x), chan: 2 (over core).
Axes of the slice: x: 2, y: 2, z: 4, core: 2. Of those that a mesh axis runs over, the one named last changes fastest.
Arguments:
- frames_in: bfloat16 [48, 8, 64, 128], P(('parts', 'tm'), 'axial'), parts along dimension 0, may hold values from -6 to 6
- spatial_weight: bfloat16 [6, 3, 64, 144], P('parts', None, None, 'chan'), parts along dimension 0, may hold values from -0.25 to 0.25
- temporal_weight: bfloat16 [6, 144, 64], P('parts', 'chan'), parts along dimension 0, may hold values from -0.3125 to 0.3125
- upstream: bfloat16 [48, 8, 64, 128], P(('parts', 'tm'), 'axial'), parts along dimension 0, may hold values from -6 to 6
Outputs:
- output: bfloat16 [48, 8, 64, 128], P(('parts', 'tm'), 'axial', 'chan'), parts along dimension 0
- input_grad: bfloat16 [48, 8, 64, 128], P(('parts', 'tm'), 'axial', 'chan'), parts along dimension 0
- spatial_grad: float32 [6, 3, 64, 144], P('parts', None, None, 'chan'), parts along dimension 0
- temporal_grad: float32 [6, 144, 64], P('parts', 'chan'), parts along dimension 0
There are 2 independent parts, one for each index of `parts`. A program takes and returns all parts, laid end to end along the dimension named above; each array names one. Nothing has to cross between parts.
All inputs are finite; a program needn't handle non-finite values.
Results may differ from a plain program's by a relative error of at most 0.009.
Values may be sent and summed in bfloat16 or wider, within the bound.
A program may use at most 64 MiB of HBM per device.

v0:
```python
import math

import jax
import jax.numpy as jnp
from jax import lax
from jax.sharding import PartitionSpec as P


def extended_2(block, sides, width, periodic):
    for axis, dim in sides:
        count = lax.axis_size(axis)
        forward = [(i, i + 1) for i in range(count - 1)]
        if periodic:
            forward.append((count - 1, 0))
        backward = [(target, source) for source, target in forward]
        low = lax.ppermute(
            lax.slice_in_dim(block, block.shape[dim] - width, None, axis=dim), axis, forward
        )
        high = lax.ppermute(lax.slice_in_dim(block, 0, width, axis=dim), axis, backward)
        block = jnp.concatenate([low, block, high], axis=dim)
    return block


def spatial_conv(padded_rows, kernel):
    return lax.conv_general_dilated(
        padded_rows,
        kernel,
        (1, 1),
        ((0, 0), (1, 1)),
        dimension_numbers=("NHCW", "HWIO", "NHCW"),
        preferred_element_type=jnp.float32,
    )


def temporal_conv(hidden_wide, weight):
    frame_count = hidden_wide.shape[0] - 2
    summed = None
    for offset in range(3):
        contrib = jnp.einsum(
            "fhmw,mc->fhcw",
            hidden_wide[offset : offset + frame_count],
            weight[offset],
            preferred_element_type=jnp.float32,
        )
        summed = contrib if summed is None else summed + contrib
    return summed


def shards(frames_in, spatial_weight, temporal_weight, upstream):
    frame_dev, row_dev, channels, width_dev = frames_in.shape
    mid_share = temporal_weight.shape[1]
    axial_count = lax.axis_size("axial")
    core_count = lax.axis_size("chan")
    factor = 1.0 / math.sqrt(frame_dev * lax.axis_size("tm") * row_dev * axial_count * width_dev)
    spatial_kernel, temporal_kernel = (
        lax.all_gather(spatial_weight, "chan", axis=3, tiled=True),
        lax.all_gather(temporal_weight, "chan", axis=1, tiled=True),
    )
    mid_local = temporal_kernel.shape[1]
    frame_local = frame_dev // core_count
    first_frame = lax.axis_index("chan") * frame_local
    own_frames = lax.dynamic_slice_in_dim(frames_in, first_frame, frame_local, 0)
    upstream_local = lax.dynamic_slice_in_dim(upstream, first_frame, frame_local, 0)
    input_rows = extended_2(own_frames, (("axial", 1),), 1, False)
    preact = spatial_conv(input_rows, spatial_kernel)
    hidden = jax.nn.silu(preact).astype(jnp.bfloat16)
    stacked = jnp.concatenate([hidden, upstream_local], axis=2)
    extended = extended_2(stacked, ((("tm", "chan"), 0),), 1, True)
    hidden_wide = extended[:, :, :mid_local]
    upstream_wide = extended[:, :, mid_local:]
    output_full = temporal_conv(hidden_wide, temporal_kernel).astype(jnp.bfloat16)
    temporal_grad = factor * jnp.stack(
        [
            jnp.einsum(
                "fhmw,fhcw->mc",
                hidden_wide[offset : offset + frame_local],
                upstream_local,
                preferred_element_type=jnp.float32,
            )
            for offset in range(3)
        ]
    )
    grad_act = None
    for offset in range(3):
        contrib = jnp.einsum(
            "fhcw,mc->fhmw",
            upstream_wide[2 - offset : 2 - offset + frame_local],
            temporal_kernel[offset],
            preferred_element_type=jnp.float32,
        )
        grad_act = contrib if grad_act is None else grad_act + contrib
    sigma = jax.nn.sigmoid(preact)
    grad_pre = (grad_act * sigma * (1.0 + preact * (1.0 - sigma))).astype(jnp.bfloat16)
    grad_padded = extended_2(grad_pre, (("axial", 1),), 1, False)
    input_part = lax.conv_general_dilated(
        grad_padded,
        spatial_kernel[::-1, ::-1],
        (1, 1),
        ((0, 0), (1, 1)),
        dimension_numbers=("NHCW", "HWOI", "NHCW"),
        preferred_element_type=jnp.float32,
    )
    kernel_terms = lax.conv_general_dilated(
        input_rows,
        grad_pre,
        (1, 1),
        ((0, 0), (1, 1)),
        dimension_numbers=("CHNW", "IHOW", "NHCW"),
        preferred_element_type=jnp.float32,
    )
    spatial_grad = factor * jnp.transpose(kernel_terms, (1, 3, 0, 2))
    input_full = input_part.astype(jnp.bfloat16)
    output, input_grad = (
        lax.all_to_all(output_full, "chan", split_axis=2, concat_axis=0, tiled=True),
        lax.all_to_all(input_full, "chan", split_axis=2, concat_axis=0, tiled=True),
    )
    spatial_total, temporal_total = lax.psum((spatial_grad, temporal_grad), ("tm", "axial", "chan"))
    mid_start = lax.axis_index("chan") * mid_share
    spatial_grad = lax.dynamic_slice_in_dim(spatial_total, mid_start, mid_share, 3)
    temporal_grad = lax.dynamic_slice_in_dim(temporal_total, mid_start, mid_share, 1)
    return (output, input_grad, spatial_grad, temporal_grad)


def solution(mesh):
    placed = (
        P(("parts", "tm"), "axial", None, None),
        P("parts", None, None, "chan"),
        P("parts", "chan", None),
        P(("parts", "tm"), "axial", None, None),
    )
    return jax.shard_map(
        shards,
        mesh=mesh,
        in_specs=placed,
        out_specs=(
            P(("parts", "tm"), "axial", "chan", None),
            P(("parts", "tm"), "axial", "chan", None),
            P("parts", None, None, "chan"),
            P("parts", "chan", None),
        ),
        check_vma=False,
    )
```

profile of v0, /device:TPU:0, one launch (start us, length us, event | category | flops | bytes accessed | tf_op | source)
XLA Modules:
  0.0 171.0 jit_solution(202611430970531133)
XLA Ops:
  7.3 0.9 constant_dynamic-slice_fusion.1
  8.2 4.9 %collective-permute-start = (bf16[3,1,64,128]{3,2,1,0:T(8,128)(2,1)S(1)}, bf16[3,1,64,128]{3,2,1,0:T(8,128)(2,1)S(1)}, u32[]{:S(2)}, u32[]{:S(2)}) collective-permute-start(bf16[3,1,64,128]{3,2,1,0:T(8,128)(2,1)S(1)} %get-tuple-element.15), channel_id=1, source_target_pairs={{0,2},{1,3},{4,6},{5,7},{8,10},{9,11},{12,14},{13,15},{16,18},{17,... | collective-permute-start | bytes 147464 | tf_op jit(solution)/shard_map/ppermute | solution.py:16
  13.0 1.3 collective-permute-start.1
  14.3 0.9 copy.76
  15.2 1.9 %all_gather.7 = bf16[3,144,64]{2,0,1:T(4,128)(2,1)S(1)} all-gather(bf16[3,72,64]{2,0,1:T(4,128)(2,1)S(1)} %copy.76), channel_id=1, replica_groups=mesh['parts'=2,'tm'=4,'axial'=2,'chan'=2] {'chan'}, dimensions={1}, use_global_device_ids=true | all-gather | bytes 82944 | tf_op jit(solution)/shard_map/all_gather | solution.py:57
  17.2 0.2 fusion.54
  17.3 0.1 copy.103
  17.5 1.2 fusion.42
  18.7 0.1 copy.101
  18.8 0.1 copy.104
  18.9 0.2 copy.72
  19.1 2.1 %all_gather.6 = bf16[3,3,64,144]{2,1,0,3:T(4,128)(2,1)S(1)} all-gather(bf16[3,3,64,72]{2,1,0,3:T(4,128)(2,1)S(1)} %copy.72), channel_id=1, replica_groups=mesh['parts'=2,'tm'=4,'axial'=2,'chan'=2] {'chan'}, dimensions={3}, use_global_device_ids=true | all-gather | bytes 248832 | tf_op jit(solution)/shard_map/all_gather | solution.py:56
  21.2 0.3 copy.73
  21.6 1.3 copy.93
  22.9 0.3 copy.107
  23.2 0.2 pad.clone
  23.4 0.2 reshape.10
  23.7 0.4 fusion.20
  24.1 2.6 %add_divide_fusion = (f32[4,24,17,144]{3,1,2,0:T(8,128)S(1)}, bf16[4,24,17,144]{3,1,2,0:T(8,128)(2,1)}, f32[4,24,17,144]{3,1,2,0:T(8,128)}) fusion(pred[24,17]{0,1:T(8,128)(4,1)S(1)} %copy-done.16, bf16[3,3,64,144]{3,2,1,0:T(8,128)(2,1)S(1)} %copy.73, bf16[6,64,3,8,19]{1,4,3,2,0:T(8,128)(2,1)S(1)} %fusion.20), kind=kOutput, calls=%fused_computation.7 | convolution fusion | flops 272844288 | bytes 2866584 | tf_op jit(solution)/shard_map/conv_general_dilated | solution.py:25
  26.7 0.6 copy.82
  27.4 0.3 slice.87
  27.7 1.0 copy.105
  28.6 1.5 copy.74
  30.1 1.2 slice.82
  31.3 1.5 copy.102
  32.8 0.9 convolution_bitcast_fusion.1
  33.7 0.8 pad_maximum_fusion.3
  34.5 0.2 collective-permute-start.2
  34.6 3.4 %collective-permute-start.3 = (bf16[1,4,208,128]{3,2,1,0:T(8,128)(2,1)}, bf16[1,4,208,128]{3,2,1,0:T(8,128)(2,1)}, u32[]{:S(2)}, u32[]{:S(2)}) collective-permute-start(bf16[1,4,208,128]{3,2,1,0:T(8,128)(2,1)} %get-tuple-element.12), channel_id=1, source_target_pairs={{1,0},{4,1},{5,4},{8,5},{9,8},{12,9},{13,12},{0,13},{3,2},{6,3},{7... | collective-permute-start | bytes 638984 | tf_op jit(solution)/shard_map/ppermute | solution.py:19
  38.0 0.6 copy.84
  38.7 0.3 slice.88
  39.0 1.5 copy.106
  40.5 1.7 fusion.44
  42.2 2.1 %maximum_maximum_fusion = (bf16[4,4,208,128]{3,2,1,0:T(8,128)(2,1)}, bf16[4,4,208,128]{3,2,1,0:T(8,128)(2,1)S(1)}) fusion(bf16[3,4,64,128]{3,2,1,0:T(8,128)(2,1)S(1)} %constant_dynamic-slice_fusion.4, bf16[3,4,144,128]{3,2,1,0:T(8,128)(2,1)S(1)} %bitcast.111, bf16[1,4,208,128]{3,2,1,0:T(8,128)(2,1)} %collective-permute-done.2, ...), kind=kLoop, calls=%fused_computation.28 | loop fusion | flops 5111808 | bytes 2768896 | tf_op jit(solution)/shard_map/concatenate | solution.py:20
  44.4 0.9 convolution_bitcast_fusion
  45.3 1.0 fusion.25
  46.2 1.1 fusion.29
  47.4 1.2 fusion.10
  48.7 1.4 copy.94
  50.1 0.3 convolution_bitcast_fusion.2
  50.4 0.2 fusion.19
  50.6 0.2 copy.80
  50.7 5.1 %all_to_all.36 = bf16[3,4,64,128]{3,1,0,2:T(4,128)(2,1)S(1)} all-to-all(bf16[3,4,64,128]{3,1,0,2:T(4,128)(2,1)S(1)} %copy.80), channel_id=1, replica_groups=mesh['parts'=2,'tm'=4,'axial'=2,'chan'=2] {'chan'}, dimensions={2} | all-to-all | bytes 393216 | tf_op jit(solution)/shard_map/all_to_all | solution.py:114
  55.9 0.7 copy.81
  56.6 4.5 %collective-permute-start.4 = (bf16[3,1,144,128]{3,2,1,0:T(8,128)(2,1)S(1)}, bf16[3,1,144,128]{3,2,1,0:T(8,128)(2,1)S(1)}, u32[]{:S(2)}, u32[]{:S(2)}) collective-permute-start(bf16[3,1,144,128]{3,2,1,0:T(8,128)(2,1)S(1)} %get-tuple-element.13), channel_id=1, source_target_pairs={{0,2},{1,3},{4,6},{5,7},{8,10},{9,11},{12,14},{13,15},{16,18},{17,... | collective-permute-start | bytes 331784 | tf_op jit(solution)/shard_map/ppermute | solution.py:16
  61.2 1.6 collective-permute-start.5
  62.8 3.4 %convolution_multiply_fusion = f32[3,3,64,144]{3,2,1,0:T(8,128)} fusion(bf16[3,6,64,128]{2,0,3,1:T(4,128)(2,1)S(1)} %copy-done.8, bf16[3,4,144,128]{2,0,3,1:T(4,128)(2,1)S(1)} %copy-done.7), kind=kOutput, calls=%fused_computation.19 | convolution fusion | flops 253559808 | bytes 1069056 | tf_op jit(solution)/shard_map/transpose | solution.py:111
  66.2 0.7 maximum_multiply_fusion
  67.0 1.1 collective-permute-done.5
  68.0 0.1 maximum_bitcast_fusion
  68.1 0.6 copy.108
  68.7 0.5 pad.2.clone
  69.2 0.5 reshape.17
  69.9 0.7 fusion.1
  70.5 0.3 copy-done.10
  70.8 2.1 %fusion.14 = bf16[4,24,17,64]{3,1,2,0:T(8,128)(2,1)S(1)} fusion(bf16[3,3,64,144]{3,2,1,0:T(8,128)(2,1)S(1)} %copy-done.10, bf16[6,144,3,8,19]{1,4,3,2,0:T(8,128)(2,1)S(1)} %fusion.1, pred[24,17]{0,1:T(8,128)(4,1)S(1)} %copy-done.17), kind=kOutput, calls=%fused_computation.18 | convolution fusion | flops 270938112 | bytes 1163160 | tf_op jit(solution)/shard_map/conv_general_dilated | solution.py:95
  72.9 0.2 copy.89
  73.1 0.1 slice_bitcast_fusion
  73.2 0.2 copy.90
  73.5 3.9 %all_to_all.37 = bf16[3,4,64,128]{3,1,0,2:T(4,128)(2,1)S(1)} all-to-all(bf16[3,4,64,128]{3,1,0,2:T(4,128)(2,1)S(1)} %copy.90), channel_id=1, replica_groups=mesh['parts'=2,'tm'=4,'axial'=2,'chan'=2] {'chan'}, dimensions={2} | all-to-all | bytes 393216 | tf_op jit(solution)/shard_map/all_to_all | solution.py:115
  77.4 0.7 copy.92
  78.1 82.5 %all-reduce.3.cloned.1.call-done = (f32[3,3,64,144]{3,2,1,0:T(8,128)}, f32[3,144,64]{1,2,0:T(8,128)}) async-done(((f32[3,3,64,144]{3,2,1,0:T(8,128)}, f32[3,144,64]{1,2,0:T(8,128)}), (f32[3,3,64,144]{3,2,1,0:T(8,128)}, f32[3,144,64]{1,2,0:T(8,128)})) %all-reduce.3.cloned.1.call-update) | async-done | bytes 442384 | tf_op jit(solution)/shard_map/psum | solution.py:117
  160.6 1.9 %constant_dynamic-slice_fusion.3 = f32[3,3,64,72]{3,2,1,0:T(8,128)} fusion(f32[3,3,64,144]{3,2,1,0:T(8,128)} %get-tuple-element.4, s32[]{:T(128)S(6)} %select_n.9), kind=kLoop, calls=%fused_computation.66 | loop fusion | bytes 331780 | tf_op jit(solution)/shard_map/dynamic_slice | solution.py:119
  162.5 1.7 constant_dynamic-slice_fusion.2
  (49 shorter events, 0.4 us)
Async XLA Ops:
  7.2 10.2 %copy-start = (bf16[6,4,64,128]{3,2,1,0:T(8,128)(2,1)S(1)}, bf16[6,4,64,128]{3,2,1,0:T(8,128)(2,1)}, u32[]{:S(2)}) copy-start(bf16[6,4,64,128]{3,2,1,0:T(8,128)(2,1)} %param.7) | copy-start | bytes 1179652
  7.2 11.5 %copy-start.13 = (bf16[6,4,64,128]{3,2,1,0:T(8,128)(2,1)S(1)}, bf16[6,4,64,128]{3,2,1,0:T(8,128)(2,1)}, u32[]{:S(2)}) copy-start(bf16[6,4,64,128]{3,2,1,0:T(8,128)(2,1)} %param.4) | copy-start | bytes 1179652
  7.2 11.7 %copy-start.14 = (bf16[3,3,64,72]{3,2,1,0:T(8,128)(2,1)S(1)}, bf16[3,3,64,72]{3,2,1,0:T(8,128)(2,1)}, u32[]{:S(2)}) copy-start(bf16[3,3,64,72]{3,2,1,0:T(8,128)(2,1)} %param.5) | copy-start | bytes 248836
  7.2 153.4 %all-reduce.3.cloned.1.call-start = ((), (), s32[]{:S(2)}) async-start(), calls=%async_computation.2 | async-start | bytes 1572864 | tf_op jit(solution)/shard_map/psum | solution.py:117
  8.2 13.4 %collective-permute-start = (bf16[3,1,64,128]{3,2,1,0:T(8,128)(2,1)S(1)}, bf16[3,1,64,128]{3,2,1,0:T(8,128)(2,1)S(1)}, u32[]{:S(2)}, u32[]{:S(2)}) collective-permute-start(bf16[3,1,64,128]{3,2,1,0:T(8,128)(2,1)S(1)} %get-tuple-element.15), channel_id=1, source_target_pairs={{0,2},{1,3},{4,6},{5,7},{8,10},{9,11},{12,14},{13,15},{16,18},{17,... | collective-permute-start | bytes 147464 | tf_op jit(solution)/shard_map/ppermute | solution.py:16
  13.0 8.5 %collective-permute-start.1 = (bf16[3,1,64,128]{3,2,1,0:T(8,128)(2,1)S(1)}, bf16[3,1,64,128]{3,2,1,0:T(8,128)(2,1)S(1)}, u32[]{:S(2)}, u32[]{:S(2)}) collective-permute-start(bf16[3,1,64,128]{3,2,1,0:T(8,128)(2,1)S(1)} %get-tuple-element.16), channel_id=1, source_target_pairs={{2,0},{3,1},{6,4},{7,5},{10,8},{11,9},{14,12},{15,13},{18,16},{19,... | collective-permute-start | bytes 147464 | tf_op jit(solution)/shard_map/ppermute | solution.py:19
  17.4 1.5 copy-start.11
  21.6 2.5 %copy-start.9 = (bf16[3,3,64,144]{3,2,1,0:T(8,128)(2,1)}, bf16[3,3,64,144]{3,2,1,0:T(8,128)(2,1)S(1)}, u32[]{:S(2)}) copy-start(bf16[3,3,64,144]{3,2,1,0:T(8,128)(2,1)S(1)} %copy.73) | copy-start | bytes 497668
  23.4 0.7 copy-start.16
  32.8 5.3 %copy-start.4 = (f32[4,24,17,144]{3,1,2,0:T(8,128)S(1)}, f32[4,24,17,144]{3,1,2,0:T(8,128)}, u32[]{:S(2)}) copy-start(f32[4,24,17,144]{3,1,2,0:T(8,128)} %get-tuple-element.8) | copy-start | bytes 2820100
  34.5 7.7 %collective-permute-start.2 = (bf16[1,4,208,128]{3,2,1,0:T(8,128)(2,1)}, bf16[1,4,208,128]{3,2,1,0:T(8,128)(2,1)}, u32[]{:S(2)}, u32[]{:S(2)}) collective-permute-start(bf16[1,4,208,128]{3,2,1,0:T(8,128)(2,1)} %get-tuple-element.11), channel_id=1, source_target_pairs={{0,1},{1,4},{4,5},{5,8},{8,9},{9,12},{12,13},{13,0},{2,3},{3,6},{6... | collective-permute-start | bytes 638984 | tf_op jit(solution)/shard_map/ppermute | solution.py:16
  34.6 7.6 %collective-permute-start.3 = (bf16[1,4,208,128]{3,2,1,0:T(8,128)(2,1)}, bf16[1,4,208,128]{3,2,1,0:T(8,128)(2,1)}, u32[]{:S(2)}, u32[]{:S(2)}) collective-permute-start(bf16[1,4,208,128]{3,2,1,0:T(8,128)(2,1)} %get-tuple-element.12), channel_id=1, source_target_pairs={{1,0},{4,1},{5,4},{8,5},{9,8},{12,9},{13,12},{0,13},{3,2},{6,3},{7... | collective-permute-start | bytes 638984 | tf_op jit(solution)/shard_map/ppermute | solution.py:19
  44.4 3.0 %copy-start.1 = (f32[4,3,128,144]{2,3,0,1:T(8,128)S(1)}, f32[4,3,128,144]{2,3,0,1:T(8,128)}, u32[]{:S(2)}) copy-start(f32[4,3,128,144]{2,3,0,1:T(8,128)} %copy.106) | copy-start | bytes 2654212
  44.4 3.0 %copy-start.2 = (f32[3,4,128,144]{2,3,1,0:T(8,128)S(1)}, f32[3,4,128,144]{2,3,1,0:T(8,128)}, u32[]{:S(2)}) copy-start(f32[3,4,128,144]{2,3,1,0:T(8,128)} %fusion.42) | copy-start | bytes 2654212
  48.6 1.5 copy-start.3
  48.6 1.7 %copy-start.5 = (f32[3,4,128,64]{2,3,1,0:T(8,128)S(1)}, f32[3,4,128,64]{2,3,1,0:T(8,128)}, u32[]{:S(2)}) copy-start(f32[3,4,128,64]{2,3,1,0:T(8,128)} %fusion.44) | copy-start | bytes 1179652
  48.6 1.7 %copy-start.6 = (f32[3,4,128,64]{2,3,1,0:T(8,128)S(1)}, f32[3,4,128,64]{2,3,1,0:T(8,128)}, u32[]{:S(2)}) copy-start(f32[3,4,128,64]{2,3,1,0:T(8,128)} %fusion.25) | copy-start | bytes 1179652
  50.1 12.7 %copy-start.7 = (bf16[3,4,144,128]{2,0,3,1:T(4,128)(2,1)S(1)}, bf16[3,4,144,128]{2,0,3,1:T(4,128)(2,1)}, u32[]{:S(2)}) copy-start(bf16[3,4,144,128]{2,0,3,1:T(4,128)(2,1)} %copy.94) | copy-start | bytes 1327108
  50.1 12.7 %copy-start.8 = (bf16[3,6,64,128]{2,0,3,1:T(4,128)(2,1)S(1)}, bf16[3,6,64,128]{2,0,3,1:T(4,128)(2,1)}, u32[]{:S(2)}) copy-start(bf16[3,6,64,128]{2,0,3,1:T(4,128)(2,1)} %copy.93) | copy-start | bytes 884740
  56.6 10.4 %collective-permute-start.4 = (bf16[3,1,144,128]{3,2,1,0:T(8,128)(2,1)S(1)}, bf16[3,1,144,128]{3,2,1,0:T(8,128)(2,1)S(1)}, u32[]{:S(2)}, u32[]{:S(2)}) collective-permute-start(bf16[3,1,144,128]{3,2,1,0:T(8,128)(2,1)S(1)} %get-tuple-element.13), channel_id=1, source_target_pairs={{0,2},{1,3},{4,6},{5,7},{8,10},{9,11},{12,14},{13,15},{16,18},{17,... | collective-permute-start | bytes 331784 | tf_op jit(solution)/shard_map/ppermute | solution.py:16
  61.1 5.1 %copy-start.12 = (f32[1,144,64]{1,2,0:T(8,128)S(1)}, f32[1,144,64]{1,2,0:T(8,128)}, u32[]{:S(2)}) copy-start(f32[1,144,64]{1,2,0:T(8,128)} %convolution_bitcast_fusion.1) | copy-start | bytes 110596
  61.2 5.1 %copy-start.15 = (f32[1,144,64]{1,2,0:T(8,128)S(1)}, f32[1,144,64]{1,2,0:T(8,128)}, u32[]{:S(2)}) copy-start(f32[1,144,64]{1,2,0:T(8,128)} %convolution_bitcast_fusion) | copy-start | bytes 110596
  61.2 6.9 %collective-permute-start.5 = (bf16[3,1,144,128]{3,2,1,0:T(8,128)(2,1)S(1)}, bf16[3,1,144,128]{3,2,1,0:T(8,128)(2,1)S(1)}, u32[]{:S(2)}, u32[]{:S(2)}) collective-permute-start(bf16[3,1,144,128]{3,2,1,0:T(8,128)(2,1)S(1)} %get-tuple-element.14), channel_id=1, source_target_pairs={{2,0},{3,1},{6,4},{7,5},{10,8},{11,9},{14,12},{15,13},{18,16},{19,... | collective-permute-start | bytes 331784 | tf_op jit(solution)/shard_map/ppermute | solution.py:19
  69.9 1.0 copy-start.10
  69.9 1.0 copy-start.17
Sparse Core Ops, SparseCore 0:
  67.1 93.4 all-reduce.2
where the time goes:
time: 172 us; the launch traced here: 171 us
  waiting for transfers between devices  83.6 us (49%)
  local copies, waits for them, and re-layouts  22.5 us (13%)
  matrix products  16.7 us (10%)
  starting transfers between devices  15.9 us (9%)
  between operations  14.6 us (8%)
  blocking collectives  13.1 us (8%)
  other arithmetic  4.78 us (3%)
    psum x1, waiting for transfers between devices, shards(): lax.psum((spatial_grad, temporal_grad), ('tm', 'axial', 'chan'))  82.5 us
    ppermute x3, starting transfers between devices, extended_2(): lax.ppermute(lax.slice_in_dim(block, block.shape[dim] - width, None, axis...  9.55 us
    unnamed x46, local copies, waits for them, and re-layouts  6.65 us
    ppermute x3, starting transfers between devices, extended_2(): lax.ppermute(lax.slice_in_dim(block, 0, width, axis=dim), axis, backward)  6.29 us
    all_to_all x1, blocking collectives, shards(): lax.all_to_all(output_full, 'chan', split_axis=2, concat_axis=0, tiled=True)  5.14 us
    all_to_all x1, blocking collectives, shards(): lax.all_to_all(input_full, 'chan', split_axis=2, concat_axis=0, tiled=True)  3.89 us
    dot_general x3, matrix products, shards(): jnp.einsum('fhcw,mc->fhmw', upstream_wide[2 - offset:2 - offset + frame_l...  3.59 us
  transfers between devices with their start and end apart: 7, of which 2 were waited for; matrix products, arithmetic and copies ran while one was open for 10% of the time, Pallas kernels for 0%

commit v1 on v0

v1 whole, which is shorter than its diff:
```python
import functools
import math

import jax
import jax.numpy as jnp
from jax import lax
from jax.experimental import pallas as pl
from jax.experimental.pallas import tpu as pltpu
from jax.sharding import PartitionSpec as P

MESH = pl.DeviceIdType.MESH
F32 = jnp.float32
BF16 = jnp.bfloat16
NT = (((1,), (1,)), ((), ()))


def mm(a, b):
    return jnp.dot(a, b, preferred_element_type=F32)


def mm_nt(a, b):
    return lax.dot_general(a, b, NT, preferred_element_type=F32)


def shifted(block, step):
    if step == 0:
        return block
    width = block.shape[1]
    lane = lax.broadcasted_iota(jnp.int32, block.shape, 1)
    edge = 0 if step > 0 else width - 1
    return jnp.where(lane == edge, 0.0, pltpu.roll(block, step % width, axis=1))


def kernel(
    dims, x, u, wf, wi, tg, to, out, ig, sg, tgrad,
    xh, uh, hid, gs, gh, ga, o_own, o_send, o_recv, i_own, i_send, i_recv,
    acc, rs_send, rs_recv, red,
    xs_sem, xr_sem, us_sem, ur_sem, hs_sem, hr_sem, gs_sem, gr_sem,
    os_sem, or_sem, is_sem, ir_sem, rss_sem, rsr_sem, ags_sem, agr_sem,
):
    F, H, C, W, M, MP, T, A, factor, owners, rp = dims
    CS = C // 2
    n = T * A
    t, a, ch = lax.axis_index("tm"), lax.axis_index("axial"), lax.axis_index("chan")
    oc = 1 - ch
    g = t * A + a
    prev_t, next_t = lax.rem(t + T - 1, T), lax.rem(t + 1, T)

    def peer(d):
        p = lax.rem(g + d, n)
        return p, {"tm": p // A, "axial": lax.rem(p, A)}

    barrier = pltpu.get_barrier_semaphore()
    for d in range(1, n):
        pl.semaphore_signal(barrier, inc=1, device_id=peer(d)[1], device_id_type=MESH)
    pl.semaphore_signal(barrier, inc=1, device_id={"chan": oc}, device_id_type=MESH)
    acc[...] = jnp.zeros_like(acc)
    pl.semaphore_wait(barrier, n)

    def remote(src, dst, s, r, dev):
        return pltpu.make_async_remote_copy(
            src_ref=src, dst_ref=dst, send_sem=s, recv_sem=r, device_id=dev, device_id_type=MESH
        )

    up_dev = {"axial": jnp.maximum(a - 1, 0)}
    down_dev = {"axial": jnp.minimum(a + 1, A - 1)}
    has_up, has_down = a > 0, a < A - 1
    x_down = remote(x.at[:, H - 1], xh.at[0], xs_sem.at[0], xr_sem.at[0], down_dev)
    x_up = remote(x.at[:, 0], xh.at[1], xs_sem.at[1], xr_sem.at[1], up_dev)
    u_next = remote(u.at[F - 1], uh.at[0], us_sem.at[0], ur_sem.at[0], {"tm": next_t})
    u_prev = remote(u.at[0], uh.at[1], us_sem.at[1], ur_sem.at[1], {"tm": prev_t})

    @pl.when(has_down)
    def _():
        x_down.start()

    @pl.when(has_up)
    def _():
        x_up.start()

    u_next.start()
    u_prev.start()

    def lanes(rows):
        return jnp.concatenate(rows, axis=1)

    def u_at(f, h):
        if f < 0:
            return uh[0, h]
        if f >= F:
            return uh[1, h]
        return u[f, h]

    def u_stack(f):
        return lanes([jnp.concatenate([u_at(f - 1, h), u_at(f, h), u_at(f + 1, h)], axis=0) for h in range(H)])

    for f in range(1, F - 1):
        ga[f] = mm(tg[...], u_stack(f))

    @pl.when(jnp.logical_not(has_up))
    def _():
        xh[0] = jnp.zeros((F, C, W), BF16)
        gh[0] = jnp.zeros((F, MP, W), BF16)

    @pl.when(jnp.logical_not(has_down))
    def _():
        xh[1] = jnp.zeros((F, C, W), BF16)
        gh[1] = jnp.zeros((F, MP, W), BF16)

    u_next.wait_recv()
    u_prev.wait_recv()
    for f in (0, F - 1):
        ga[f] = mm(tg[...], u_stack(f))

    @pl.when(has_up)
    def _():
        x_down.wait_recv()

    @pl.when(has_down)
    def _():
        x_up.wait_recv()

    h_next = remote(hid.at[F], hid.at[0], hs_sem.at[0], hr_sem.at[0], {"tm": next_t})
    h_prev = remote(hid.at[1], hid.at[F + 1], hs_sem.at[1], hr_sem.at[1], {"tm": prev_t})

    def g_down(f):
        return remote(gs.at[f, H - 1, 1], gh.at[0, f], gs_sem.at[0, f], gr_sem.at[0, f], down_dev)

    def g_up(f):
        return remote(gs.at[f, 0, 1], gh.at[1, f], gs_sem.at[1, f], gr_sem.at[1, f], up_dev)

    for f in [0, F - 1] + list(range(1, F - 1)):
        rows = [xh[0, f]] + [x[f, h] for h in range(H)] + [xh[1, f]]
        xst = lanes([jnp.concatenate(rows[h : h + 3], axis=0) for h in range(H)])
        y = mm(wf[...], xst)
        hs, gsh = [], []
        for h in range(H):
            sl = slice(h * W, (h + 1) * W)
            pre = (
                shifted(y[0:MP, sl], 1) + y[MP : 2 * MP, sl] + shifted(y[2 * MP :, sl], -1)
            )
            sig = 1.0 / (1.0 + jnp.exp(-pre))
            hv = (pre * sig).astype(BF16)
            hid[f + 1, h] = hv
            hs.append(hv)
            gv = ga[f, :, sl] * sig * (1.0 + pre * (1.0 - sig))
            trio = [shifted(gv, j - 1).astype(BF16) for j in range(3)]
            for j in range(3):
                gs[f, h, j] = trio[j]
            gsh.append(jnp.concatenate(trio, axis=0))
        if f == 0:
            h_prev.start()
        if f == F - 1:
            h_next.start()

        @pl.when(has_down)
        def _():
            g_down(f).start()

        @pl.when(has_up)
        def _():
            g_up(f).start()

        acc[:, 0 : 3 * MP] += mm_nt(xst, lanes(gsh))
        acc[:, T0 : T0 + MP] += mm_nt(u_stack(f), lanes(hs))

    for p in range(owners):
        rs_send[p] = (acc[p * rp : (p + 1) * rp] * factor).astype(BF16)

    def rs_copy(d):
        p, dev = peer(d)
        return remote(rs_send.at[lax.rem(p, owners)], rs_recv.at[d - 1], rss_sem.at[d - 1], rsr_sem.at[d - 1], dev)

    def guarded(cond, do):
        if owners == n:
            do()
        else:
            pl.when(cond)(do)

    for d in range(1, n):
        guarded(peer(d)[0] < owners, lambda: rs_copy(d).start())

    own_rows = pl.ds(pl.multiple_of(ch * CS, CS), CS)
    far_rows = pl.ds(pl.multiple_of(oc * CS, CS), CS)
    to2 = jnp.concatenate([to[own_rows, :], to[far_rows, :]], axis=0)

    def o_copy(f):
        return remote(o_send.at[f], o_recv.at[f], os_sem.at[f], or_sem.at[f], {"chan": oc})

    def i_copy(f):
        return remote(i_send.at[f], i_recv.at[f], is_sem.at[f], ir_sem.at[f], {"chan": oc})

    for f in list(range(1, F - 1)) + [0, F - 1]:
        if f == 0:
            h_next.wait_recv()
        if f == F - 1:
            h_prev.wait_recv()
        st = lanes([jnp.concatenate([hid[f + k, h] for k in range(3)], axis=0) for h in range(H)])
        y = mm(to2, st)
        for h in range(H):
            sl = slice(h * W, (h + 1) * W)
            o_own[f, h] = y[:CS, sl]
            o_send[f, h] = y[CS:, sl].astype(BF16)
        o_copy(f).start()

    def ag_copy(d):
        _, dev = peer(d)
        mine = red.at[lax.rem(g, owners)]
        return remote(mine, mine, ags_sem.at[d - 1], agr_sem.at[d - 1], dev)

    def reduce_piece():
        total = acc[pl.ds(pl.multiple_of(lax.rem(g, owners) * rp, 8), rp), :] * factor
        for d in range(1, n):
            rs_copy(d).wait_recv()
            total = total + rs_recv[d - 1].astype(F32)
        red[lax.rem(g, owners)] = total.astype(BF16)
        for d in range(1, n):
            ag_copy(d).start()

    wi2 = jnp.concatenate(
        [wi[i, own_rows, :] for i in range(3)] + [wi[i, far_rows, :] for i in range(3)], axis=0
    )
    for f in range(F):
        if f == F // 2:
            guarded(g < owners, reduce_piece)

        @pl.when(has_up)
        def _():
            g_down(f).wait_recv()

        @pl.when(has_down)
        def _():
            g_up(f).wait_recv()

        halo = []
        for side in range(2):
            gv = gh[side, f].astype(F32)
            halo.append(jnp.concatenate([shifted(gv, j - 1).astype(BF16) for j in range(3)], axis=0))
        body = [jnp.concatenate([gs[f, h, j] for j in range(3)], axis=0) for h in range(H)]
        y = mm(wi2, lanes([halo[0]] + body + [halo[1]]))
        for h in range(H):
            def part(base):
                s = None
                for i in range(3):
                    e = h + 2 - i
                    v = y[base + i * CS : base + (i + 1) * CS, e * W : (e + 1) * W]
                    s = v if s is None else s + v
                return s

            i_own[f, h] = part(0)
            i_send[f, h] = part(3 * CS).astype(BF16)
        i_copy(f).start()

    for f in range(F):
        o_copy(f).wait_recv()
        out[f] = (o_own[f] + o_recv[f].astype(F32)).astype(BF16)
    for f in range(F):
        i_copy(f).wait_recv()
        ig[f] = (i_own[f] + i_recv[f].astype(F32)).astype(BF16)

    for d in range(1, n):
        src = lax.rem(g + n - d, n)

        def arrive():
            dst = red.at[lax.rem(src, owners)]
            remote(dst, dst, ags_sem.at[d - 1], agr_sem.at[d - 1], peer(n - d)[1]).wait_recv()

        guarded(src < owners, arrive)
    total = jnp.concatenate([red[p].astype(F32) for p in range(owners)], axis=0)
    for i in range(3):
        for j in range(3):
            sg[i, j] = total[i * C : (i + 1) * C, j * MP : j * MP + M]
    for k in range(3):
        tgrad[2 - k] = jnp.transpose(total[k * C : (k + 1) * C, T0 : T0 + 128])[:M]

    @pl.when(has_down)
    def _():
        x_down.wait_send()
        for f in range(F):
            g_down(f).wait_send()

    @pl.when(has_up)
    def _():
        x_up.wait_send()
        for f in range(F):
            g_up(f).wait_send()

    u_next.wait_send()
    u_prev.wait_send()
    h_next.wait_send()
    h_prev.wait_send()
    for f in range(F):
        o_copy(f).wait_send()
        i_copy(f).wait_send()
    for d in range(1, n):
        guarded(peer(d)[0] < owners, lambda: rs_copy(d).wait_send())
        guarded(g < owners, lambda: ag_copy(d).wait_send())


T0 = 256


def shards(x, sw, tw, u):
    F, H, C, W = x.shape
    M = tw.shape[1]
    MP = -(-M // 16) * 16
    T, A = lax.axis_size("tm"), lax.axis_size("axial")
    n = T * A
    factor = 1.0 / math.sqrt(F * T * H * A * W)
    R, L = 3 * C, T0 + 128
    rp = next(r for r in range(8, R + 1, 8) if R % r == 0 and R // r <= n)
    owners = R // rp
    CS = C // 2
    swp = jnp.pad(sw, ((0, 0), (0, 0), (0, 0), (0, MP - M)))
    twp = jnp.pad(tw, ((0, 0), (0, MP - M), (0, 0)))
    wf = jnp.transpose(swp, (1, 3, 0, 2)).reshape(3 * MP, 3 * C)
    wi = jnp.transpose(swp, (0, 2, 1, 3)).reshape(3, C, 3 * MP)
    tg = jnp.transpose(twp[::-1], (1, 0, 2)).reshape(MP, 3 * C)
    to = jnp.transpose(twp, (2, 0, 1)).reshape(C, 3 * MP)
    vm = pl.BlockSpec(memory_space=pltpu.VMEM)
    dma = pltpu.SemaphoreType.DMA
    return pl.pallas_call(
        functools.partial(kernel, (F, H, C, W, M, MP, T, A, factor, owners, rp)),
        out_shape=(
            jax.ShapeDtypeStruct((F, H, CS, W), BF16),
            jax.ShapeDtypeStruct((F, H, CS, W), BF16),
            jax.ShapeDtypeStruct((3, 3, C, M), F32),
            jax.ShapeDtypeStruct((3, M, C), F32),
        ),
        in_specs=[vm] * 6,
        out_specs=[vm] * 4,
        scratch_shapes=[
            pltpu.VMEM((2, F, C, W), BF16),
            pltpu.VMEM((2, H, C, W), BF16),
            pltpu.VMEM((F + 2, H, MP, W), BF16),
            pltpu.VMEM((F, H, 3, MP, W), BF16),
            pltpu.VMEM((2, F, MP, W), BF16),
            pltpu.VMEM((F, MP, H * W), F32),
            pltpu.VMEM((F, H, CS, W), F32),
            pltpu.VMEM((F, H, CS, W), BF16),
            pltpu.VMEM((F, H, CS, W), BF16),
            pltpu.VMEM((F, H, CS, W), F32),
            pltpu.VMEM((F, H, CS, W), BF16),
            pltpu.VMEM((F, H, CS, W), BF16),
            pltpu.VMEM((R, L), F32),
            pltpu.VMEM((owners, rp, L), BF16),
            pltpu.VMEM((n - 1, rp, L), BF16),
            pltpu.VMEM((owners, rp, L), BF16),
            dma((2,)), dma((2,)), dma((2,)), dma((2,)), dma((2,)), dma((2,)),
            dma((2, F)), dma((2, F)),
            dma((F,)), dma((F,)), dma((F,)), dma((F,)),
            dma((n - 1,)), dma((n - 1,)), dma((n - 1,)), dma((n - 1,)),
        ],
        compiler_params=pltpu.CompilerParams(collective_id=0, has_side_effects=True),
    )(x, u, wf, wi, tg, to)


def solution(mesh):
    placed = (
        P(("parts", "tm"), "axial", None, None),
        P("parts", None, None, "chan"),
        P("parts", "chan", None),
        P(("parts", "tm"), "axial", None, None),
    )
    return jax.shard_map(
        shards,
        mesh=mesh,
        in_specs=placed,
        out_specs=(
            P(("parts", "tm"), "axial", "chan", None),
            P(("parts", "tm"), "axial", "chan", None),
            P("parts", None, None, "chan"),
            P("parts", "chan", None),
        ),
        check_vma=False,
    )
```

time: 172 us -> 36.5 us (0.21)
  waiting for transfers between devices: 83.6 us -> 0 us
  Pallas kernels: 0 us -> 26.9 us
  matrix products: 16.7 us -> 0 us
  starting transfers between devices: 15.9 us -> 0 us
  between operations: 14.6 us -> 0.69 us
  local copies, waits for them, and re-layouts: 22.5 us -> 8.7 us
  blocking collectives: 13.1 us -> 0 us
  other arithmetic: 4.78 us -> 0 us
    psum x1 -> x0, waiting for transfers between devices: 82.5 us -> none  [shards(): lax.psum((spatial_grad, temporal_grad), ('tm', 'axial', 'chan'))]
    pallas_call x0 -> x1, Pallas kernels: none -> 26.9 us  [shards(): pl.pallas_call(functools.partial(kernel, (F, H, C, W, M, MP, T, A, factor...]
    ppermute x6 -> x0, starting transfers between devices: 15.8 us -> none  [the longest x3 9.55 us: extended_2(): lax.ppermute(lax.slice_in_dim(block, block.shape[dim] - width, None, axis...]
    all_to_all x2 -> x0, blocking collectives: 9.03 us -> none  [the longest x1 5.14 us: shards(): lax.all_to_all(output_full, 'chan', split_axis=2, concat_axis=0, tiled=True)]
    dot_general x9 -> x0, matrix products: 8.52 us -> none  [the longest x3 3.59 us: shards(): jnp.einsum('fhcw,mc->fhmw', upstream_wide[2 - offset:2 - offset + frame_l...]
    convert_element_type x7 -> x0, local copies, waits for them, and re-layouts: 4.73 us -> none  [the longest x2 2.63 us: shards(): hidden = jax.nn.silu(preact).astype(jnp.bfloat16)]
    conv_general_dilated x2 -> x0, matrix products: 4.72 us -> none  [the longest x1 2.62 us: spatial_conv(): lax.conv_general_dilated(padded_rows, kernel, (1, 1), ((0, 0), (1, 1)), d...]
    all_gather x2 -> x0, blocking collectives: 4.04 us -> none  [the longest x1 2.12 us: shards(): lax.all_gather(spatial_weight, 'chan', axis=3, tiled=True)]
  transfers between devices with their start and end apart: 7 -> 0, of which waited for: 2 -> 0; matrix products, arithmetic and copies ran while one was open for 10% -> 0% of each run, Pallas kernels for 0% -> 0%
where the time goes in v1:
time: 36.5 us; the launch traced here: 36.2 us
  Pallas kernels  26.9 us (74%)
  local copies, waits for them, and re-layouts  8.7 us (24%)
  between operations  0.69 us (2%)
    pallas_call x1, Pallas kernels, shards(): pl.pallas_call(functools.partial(kernel, (F, H, C, W, M, MP, T, A, factor...  26.9 us
    unnamed x11, local copies, waits for them, and re-layouts  2.75 us
    pallas_call x1, local copies, waits for them, and re-layouts, shards(): pl.pallas_call(functools.partial(kernel, (F, H, C, W, M, MP, T, A, factor...  1.68 us
    reshape x2, local copies, waits for them, and re-layouts, shards(): wf = jnp.transpose(swp, (1, 3, 0, 2)).reshape(3 * MP, 3 * C)  1.02 us
    transpose x2, local copies, waits for them, and re-layouts, shards(): to = jnp.transpose(twp, (2, 0, 1)).reshape(C, 3 * MP)  0.86 us
    reshape x1, local copies, waits for them, and re-layouts, shards(): wi = jnp.transpose(swp, (0, 2, 1, 3)).reshape(3, C, 3 * MP)  0.78 us

profile of v1, /device:TPU:0, one launch (start us, length us, event | category | flops | bytes accessed | tf_op | source)
XLA Modules:
  0.0 36.2 jit_solution(3935812063034220975)
XLA Ops:
  0.6 0.8 %pad_bitcast_fusion.2 = (bf16[64,3,80]{2,0,1:T(8,128)(2,1)S(1)}, bf16[3,80,64]{1,2,0:T(8,128)(2,1)S(1)}) fusion(bf16[3,72,64]{1,2,0:T(8,128)(2,1)} %param.6), kind=kLoop, calls=%fused_computation.2 | loop fusion | bytes 89088 | tf_op jit(solution)/shard_map/transpose | solution.py:319
  1.5 0.0 copy-start.3
  1.5 0.7 %reshape.23.to = bf16[64,240]{1,0:T(8,128)(2,1)} reshape(bf16[64,3,80]{2,1,0:T(4,128)(2,1)S(1)} %copy.15) | data formatting | bytes 61440 | tf_op jit(solution)/shard_map/reshape | solution.py:319
  2.2 0.7 %copy.17.tg = bf16[80,192]{1,0:T(8,128)(2,1)} copy(bf16[80,192]{0,1:T(8,128)(2,1)S(1)} %bitcast.9) | data formatting | bytes 61440 | tf_op jit(solution)/shard_map/reshape | solution.py:318
  3.0 0.0 copy-done.3
  3.0 0.1 copy.14
  3.1 0.8 %reshape.21.wi = bf16[3,64,240]{2,1,0:T(8,128)(2,1)} reshape(bf16[3,64,3,80]{3,2,1,0:T(4,128)(2,1)S(1)} %copy.14) | data formatting | bytes 184320 | tf_op jit(solution)/shard_map/reshape | solution.py:317
  3.9 0.2 copy.19
  4.1 0.8 %reshape.24.wf = bf16[240,192]{1,0:T(8,128)(2,1)} reshape(bf16[3,80,3,64]{3,2,1,0:T(4,128)(2,1)S(1)} %copy.19) | data formatting | bytes 184320 | tf_op jit(solution)/shard_map/reshape | solution.py:316
  5.0 26.9 %shard_map.75 = (bf16[6,4,32,128]{3,2,1,0:T(8,128)(2,1)}, bf16[6,4,32,128]{3,2,1,0:T(8,128)(2,1)}, f32[3,3,64,72]{3,2,1,0:T(8,128)}, f32[3,72,64]{2,1,0:T(8,128)}) custom-call(bf16[6,4,64,128]{3,2,1,0:T(8,128)(2,1)} %x.5, bf16[6,4,64,128]{3,2,1,0:T(8,128)(2,1)} %u.1, bf16[240,192]{1,0:T(8,128)(2,1)} %reshape.24.wf, bf16[3,64,240]{2,1,0:T(8,128)(2,1)} %reshape.21.wi, ...), custom_call_target="tpu_custom_call" | custom-call | tf_op jit(solution)/shard_map/pallas_call | solution.py:322
  31.8 0.0 copy-start.2
  31.8 1.7 %copy.18 = f32[3,72,64]{1,2,0:T(8,128)} copy(f32[3,72,64]{2,1,0:T(8,128)} %get-tuple-element.11) | data formatting | bytes 110592 | tf_op jit(solution)/shard_map/pallas_call | solution.py:322
  33.5 0.0 copy-done.2
  33.5 0.0 copy-start.1
  33.5 0.7 %copy.24 = bf16[6,4,32,128]{3,2,1,0:T(8,128)(2,1)} copy(bf16[6,4,32,128]{3,2,1,0:T(8,128)(2,1)S(1)} %copy-done.2) | data formatting | bytes 393216
  34.2 0.3 copy-done.1
  34.5 0.0 copy-start
  34.5 0.7 %copy.25 = bf16[6,4,32,128]{3,2,1,0:T(8,128)(2,1)} copy(bf16[6,4,32,128]{3,2,1,0:T(8,128)(2,1)S(1)} %copy-done.1) | data formatting | bytes 393216
  35.2 0.4 copy-done
  35.5 0.7 %copy.26 = f32[3,3,64,72]{3,2,1,0:T(8,128)} copy(f32[3,3,64,72]{3,2,1,0:T(8,128)S(1)} %copy-done) | data formatting | bytes 331776
  (3 shorter events, 0.1 us)
Async XLA Ops:
  1.5 1.5 %copy-start.3 = (bf16[3,3,64,72]{3,2,1,0:T(8,128)(2,1)S(1)}, bf16[3,3,64,72]{3,2,1,0:T(8,128)(2,1)}, u32[]{:S(2)}) copy-start(bf16[3,3,64,72]{3,2,1,0:T(8,128)(2,1)} %param.5) | copy-start | bytes 248836
  31.8 1.7 %copy-start.2 = (bf16[6,4,32,128]{3,2,1,0:T(8,128)(2,1)S(1)}, bf16[6,4,32,128]{3,2,1,0:T(8,128)(2,1)}, u32[]{:S(2)}) copy-start(bf16[6,4,32,128]{3,2,1,0:T(8,128)(2,1)} %get-tuple-element.20) | copy-start | bytes 589828
  33.5 1.0 %copy-start.1 = (bf16[6,4,32,128]{3,2,1,0:T(8,128)(2,1)S(1)}, bf16[6,4,32,128]{3,2,1,0:T(8,128)(2,1)}, u32[]{:S(2)}) copy-start(bf16[6,4,32,128]{3,2,1,0:T(8,128)(2,1)} %get-tuple-element.21) | copy-start | bytes 589828
  34.5 1.0 %copy-start = (f32[3,3,64,72]{3,2,1,0:T(8,128)S(1)}, f32[3,3,64,72]{3,2,1,0:T(8,128)}, u32[]{:S(2)}) copy-start(f32[3,3,64,72]{3,2,1,0:T(8,128)} %get-tuple-element.22) | copy-start | bytes 497668

commit v2 on v1

--- a/solution.py
+++ b/solution.py
@@ -32,7 +32,8 @@
 
 
 def kernel(
-    dims, x, u, wf, wi, tg, to, out, ig, sg, tgrad,
+    dims, x, u, sw, tw, out, ig, sg, tgrad,
+    wf, wi, tg, to,
     xh, uh, hid, gs, gh, ga, o_own, o_send, o_recv, i_own, i_send, i_recv,
     acc, rs_send, rs_recv, red,
     xs_sem, xr_sem, us_sem, ur_sem, hs_sem, hr_sem, gs_sem, gr_sem,
@@ -50,37 +51,6 @@
         p = lax.rem(g + d, n)
         return p, {"tm": p // A, "axial": lax.rem(p, A)}
 
-    barrier = pltpu.get_barrier_semaphore()
-    for d in range(1, n):
-        pl.semaphore_signal(barrier, inc=1, device_id=peer(d)[1], device_id_type=MESH)
-    pl.semaphore_signal(barrier, inc=1, device_id={"chan": oc}, device_id_type=MESH)
-    acc[...] = jnp.zeros_like(acc)
-    pl.semaphore_wait(barrier, n)
-
-    def remote(src, dst, s, r, dev):
-        return pltpu.make_async_remote_copy(
-            src_ref=src, dst_ref=dst, send_sem=s, recv_sem=r, device_id=dev, device_id_type=MESH
-        )
-
-    up_dev = {"axial": jnp.maximum(a - 1, 0)}
-    down_dev = {"axial": jnp.minimum(a + 1, A - 1)}
-    has_up, has_down = a > 0, a < A - 1
-    x_down = remote(x.at[:, H - 1], xh.at[0], xs_sem.at[0], xr_sem.at[0], down_dev)
-    x_up = remote(x.at[:, 0], xh.at[1], xs_sem.at[1], xr_sem.at[1], up_dev)
-    u_next = remote(u.at[F - 1], uh.at[0], us_sem.at[0], ur_sem.at[0], {"tm": next_t})
-    u_prev = remote(u.at[0], uh.at[1], us_sem.at[1], ur_sem.at[1], {"tm": prev_t})
-
-    @pl.when(has_down)
-    def _():
-        x_down.start()
-
-    @pl.when(has_up)
-    def _():
-        x_up.start()
-
-    u_next.start()
-    u_prev.start()
-
     def lanes(rows):
         return jnp.concatenate(rows, axis=1)
 
@@ -94,8 +64,60 @@
     def u_stack(f):
         return lanes([jnp.concatenate([u_at(f - 1, h), u_at(f, h), u_at(f + 1, h)], axis=0) for h in range(H)])
 
-    for f in range(1, F - 1):
-        ga[f] = mm(tg[...], u_stack(f))
+    def ga_inner():
+        for f in range(1, F - 1):
+            ga[f] = mm(tg[...], u_stack(f))
+
+    barrier = pltpu.get_barrier_semaphore()
+    for d in range(1, n):
+        pl.semaphore_signal(barrier, inc=1, device_id=peer(d)[1], device_id_type=MESH)
+    pl.semaphore_signal(barrier, inc=1, device_id={"chan": oc}, device_id_type=MESH)
+    acc[...] = jnp.zeros_like(acc)
+
+    def widen(parts):
+        zero = jnp.zeros((parts[0].shape[0], MP - M), F32)
+        return jnp.concatenate([v for p in parts for v in (p.astype(F32), zero)], axis=1)
+
+    tcol = [widen([tw[k]]) for k in range(3)]
+    tg[...] = jnp.transpose(jnp.concatenate(tcol[::-1], axis=0)).astype(BF16)
+    to[...] = jnp.concatenate(tcol, axis=1).astype(BF16)
+    ga_inner()
+    wide = jnp.concatenate([widen([sw[i, j] for j in range(3)]) for i in range(3)], axis=0)
+    wf[...] = jnp.transpose(wide).astype(BF16)
+    for i in range(3):
+        wi[i] = wide[i * C : (i + 1) * C].astype(BF16)
+    pl.semaphore_wait(barrier, n)
+
+    def remote(src, dst, s, r, dev):
+        return pltpu.make_async_remote_copy(
+            src_ref=src, dst_ref=dst, send_sem=s, recv_sem=r, device_id=dev, device_id_type=MESH
+        )
+
+    up_dev = {"axial": jnp.maximum(a - 1, 0)}
+    down_dev = {"axial": jnp.minimum(a + 1, A - 1)}
+    has_up, has_down = a > 0, a < A - 1
+    def x_down(f):
+        return remote(x.at[f, H - 1], xh.at[0, f], xs_sem.at[0, f], xr_sem.at[0, f], down_dev)
+
+    def x_up(f):
+        return remote(x.at[f, 0], xh.at[1, f], xs_sem.at[1, f], xr_sem.at[1, f], up_dev)
+
+    order = [0, F - 1] + list(range(1, F - 1))
+    u_next = remote(u.at[F - 1], uh.at[0], us_sem.at[0], ur_sem.at[0], {"tm": next_t})
+    u_prev = remote(u.at[0], uh.at[1], us_sem.at[1], ur_sem.at[1], {"tm": prev_t})
+
+    @pl.when(has_down)
+    def _():
+        for f in order:
+            x_down(f).start()
+
+    @pl.when(has_up)
+    def _():
+        for f in order:
+            x_up(f).start()
+
+    u_next.start()
+    u_prev.start()
 
     @pl.when(jnp.logical_not(has_up))
     def _():
@@ -112,14 +134,6 @@
     for f in (0, F - 1):
         ga[f] = mm(tg[...], u_stack(f))
 
-    @pl.when(has_up)
-    def _():
-        x_down.wait_recv()
-
-    @pl.when(has_down)
-    def _():
-        x_up.wait_recv()
-
     h_next = remote(hid.at[F], hid.at[0], hs_sem.at[0], hr_sem.at[0], {"tm": next_t})
     h_prev = remote(hid.at[1], hid.at[F + 1], hs_sem.at[1], hr_sem.at[1], {"tm": prev_t})
 
@@ -129,7 +143,15 @@
     def g_up(f):
         return remote(gs.at[f, 0, 1], gh.at[1, f], gs_sem.at[1, f], gr_sem.at[1, f], up_dev)
 
-    for f in [0, F - 1] + list(range(1, F - 1)):
+    for f in order:
+        @pl.when(has_up)
+        def _():
+            x_down(f).wait_recv()
+
+        @pl.when(has_down)
+        def _():
+            x_up(f).wait_recv()
+
         rows = [xh[0, f]] + [x[f, h] for h in range(H)] + [xh[1, f]]
         xst = lanes([jnp.concatenate(rows[h : h + 3], axis=0) for h in range(H)])
         y = mm(wf[...], xst)
@@ -271,18 +293,18 @@
         for j in range(3):
             sg[i, j] = total[i * C : (i + 1) * C, j * MP : j * MP + M]
     for k in range(3):
-        tgrad[2 - k] = jnp.transpose(total[k * C : (k + 1) * C, T0 : T0 + 128])[:M]
+        tgrad[2 - k] = total[k * C : (k + 1) * C, T0 : T0 + M]
 
     @pl.when(has_down)
     def _():
-        x_down.wait_send()
         for f in range(F):
+            x_down(f).wait_send()
             g_down(f).wait_send()
 
     @pl.when(has_up)
     def _():
-        x_up.wait_send()
         for f in range(F):
+            x_up(f).wait_send()
             g_up(f).wait_send()
 
     u_next.wait_send()
@@ -311,25 +333,23 @@
     rp = next(r for r in range(8, R + 1, 8) if R % r == 0 and R // r <= n)
     owners = R // rp
     CS = C // 2
-    swp = jnp.pad(sw, ((0, 0), (0, 0), (0, 0), (0, MP - M)))
-    twp = jnp.pad(tw, ((0, 0), (0, MP - M), (0, 0)))
-    wf = jnp.transpose(swp, (1, 3, 0, 2)).reshape(3 * MP, 3 * C)
-    wi = jnp.transpose(swp, (0, 2, 1, 3)).reshape(3, C, 3 * MP)
-    tg = jnp.transpose(twp[::-1], (1, 0, 2)).reshape(MP, 3 * C)
-    to = jnp.transpose(twp, (2, 0, 1)).reshape(C, 3 * MP)
     vm = pl.BlockSpec(memory_space=pltpu.VMEM)
     dma = pltpu.SemaphoreType.DMA
-    return pl.pallas_call(
+    out, ig, sgrad, tgrad = pl.pallas_call(
         functools.partial(kernel, (F, H, C, W, M, MP, T, A, factor, owners, rp)),
         out_shape=(
             jax.ShapeDtypeStruct((F, H, CS, W), BF16),
             jax.ShapeDtypeStruct((F, H, CS, W), BF16),
             jax.ShapeDtypeStruct((3, 3, C, M), F32),
-            jax.ShapeDtypeStruct((3, M, C), F32),
+            jax.ShapeDtypeStruct((3, C, M), F32),
         ),
-        in_specs=[vm] * 6,
+        in_specs=[vm] * 4,
         out_specs=[vm] * 4,
         scratch_shapes=[
+            pltpu.VMEM((3 * MP, 3 * C), BF16),
+            pltpu.VMEM((3, C, 3 * MP), BF16),
+            pltpu.VMEM((MP, 3 * C), BF16),
+            pltpu.VMEM((C, 3 * MP), BF16),
             pltpu.VMEM((2, F, C, W), BF16),
             pltpu.VMEM((2, H, C, W), BF16),
             pltpu.VMEM((F + 2, H, MP, W), BF16),
@@ -346,13 +366,14 @@
             pltpu.VMEM((owners, rp, L), BF16),
             pltpu.VMEM((n - 1, rp, L), BF16),
             pltpu.VMEM((owners, rp, L), BF16),
-            dma((2,)), dma((2,)), dma((2,)), dma((2,)), dma((2,)), dma((2,)),
+            dma((2, F)), dma((2, F)), dma((2,)), dma((2,)), dma((2,)), dma((2,)),
             dma((2, F)), dma((2, F)),
             dma((F,)), dma((F,)), dma((F,)), dma((F,)),
             dma((n - 1,)), dma((n - 1,)), dma((n - 1,)), dma((n - 1,)),
         ],
         compiler_params=pltpu.CompilerParams(collective_id=0, has_side_effects=True),
-    )(x, u, wf, wi, tg, to)
+    )(x, u, sw, jnp.transpose(tw, (0, 2, 1)))
+    return out, ig, sgrad, jnp.transpose(tgrad, (0, 2, 1))
 
 
 def solution(mesh):

time: 36.5 us -> 32.4 us (0.89)
  local copies, waits for them, and re-layouts: 8.7 us -> 4.29 us
    reshape x5 -> x0, local copies, waits for them, and re-layouts: 3.24 us -> none  [the longest x2 1.02 us: shards(): wf = jnp.transpose(swp, (1, 3, 0, 2)).reshape(3 * MP, 3 * C)]
    pallas_call x1 -> x0, local copies, waits for them, and re-layouts: 1.68 us -> none  [shards(): pl.pallas_call(functools.partial(kernel, (F, H, C, W, M, MP, T, A, factor...]
    unnamed x11 -> x10, local copies, waits for them, and re-layouts: 2.75 us -> 4.29 us
    transpose x4 -> x0, local copies, waits for them, and re-layouts: 1.03 us -> none  [the longest x2 0.86 us: shards(): to = jnp.transpose(twp, (2, 0, 1)).reshape(C, 3 * MP)]
where the time goes in v2:
time: 32.4 us; the launch traced here: 32.2 us
  Pallas kernels  27.2 us (84%)
  local copies, waits for them, and re-layouts  4.29 us (13%)
  between operations  0.65 us (2%)
    pallas_call x1, Pallas kernels, shards(): pl.pallas_call(functools.partial(kernel, (F, H, C, W, M, MP, T, A, factor...  27.2 us
    unnamed x10, local copies, waits for them, and re-layouts  4.29 us

profile of v2, /device:TPU:0, one launch (start us, length us, event | category | flops | bytes accessed | tf_op | source)
XLA Modules:
  0.0 32.2 jit_solution(11838436942457779434)
XLA Ops:
  0.6 27.2 %shard_map.75 = (bf16[6,4,32,128]{3,2,1,0:T(8,128)(2,1)}, bf16[6,4,32,128]{3,2,1,0:T(8,128)(2,1)}, f32[3,3,64,72]{3,2,1,0:T(8,128)}, f32[3,64,72]{2,1,0:T(8,128)}) custom-call(bf16[6,4,64,128]{3,2,1,0:T(8,128)(2,1)} %x.1, bf16[6,4,64,128]{3,2,1,0:T(8,128)(2,1)} %u.1, bf16[3,3,64,72]{3,2,1,0:T(8,128)(2,1)} %sw.1, bf16[3,64,72]{2,1,0:T(8,128)(2,1)} %bitcast.3), custom_call_target="tpu_custom_call" | custom-call | tf_op jit(solution)/shard_map/pallas_call | solution.py:338
  27.9 0.0 copy-start.1
  27.9 1.7 %copy.12 = bf16[6,4,32,128]{3,2,1,0:T(8,128)(2,1)} copy(bf16[6,4,32,128]{3,2,1,0:T(8,128)(2,1)} %get-tuple-element.16) | data formatting | bytes 393216
  29.5 0.0 copy-done.1
  29.5 0.0 copy-start
  29.5 0.7 %copy.13 = bf16[6,4,32,128]{3,2,1,0:T(8,128)(2,1)} copy(bf16[6,4,32,128]{3,2,1,0:T(8,128)(2,1)S(1)} %copy-done.1) | data formatting | bytes 393216
  30.2 0.4 %copy-done = f32[3,3,64,72]{3,2,1,0:T(8,128)S(1)} copy-done((f32[3,3,64,72]{3,2,1,0:T(8,128)S(1)}, f32[3,3,64,72]{3,2,1,0:T(8,128)}, u32[]{:S(2)}) %copy-start) | copy-done | bytes 165912
  30.6 0.0 copy-start.2
  30.6 0.7 %copy.14 = f32[3,3,64,72]{3,2,1,0:T(8,128)} copy(f32[3,3,64,72]{3,2,1,0:T(8,128)S(1)} %copy-done) | data formatting | bytes 331776
  31.3 0.2 copy-done.2
  31.5 0.6 %copy.15 = f32[3,72,64]{1,2,0:T(8,128)} copy(f32[3,72,64]{1,2,0:T(8,128)S(1)} %bitcast.2) | data formatting | bytes 110592
Async XLA Ops:
  27.9 1.7 %copy-start.1 = (bf16[6,4,32,128]{3,2,1,0:T(8,128)(2,1)S(1)}, bf16[6,4,32,128]{3,2,1,0:T(8,128)(2,1)}, u32[]{:S(2)}) copy-start(bf16[6,4,32,128]{3,2,1,0:T(8,128)(2,1)} %get-tuple-element.17) | copy-start | bytes 589828
  29.5 1.0 %copy-start = (f32[3,3,64,72]{3,2,1,0:T(8,128)S(1)}, f32[3,3,64,72]{3,2,1,0:T(8,128)}, u32[]{:S(2)}) copy-start(f32[3,3,64,72]{3,2,1,0:T(8,128)} %get-tuple-element.18) | copy-start | bytes 497668
  30.6 1.0 %copy-start.2 = (f32[3,64,72]{2,1,0:T(8,128)S(1)}, f32[3,64,72]{2,1,0:T(8,128)}, u32[]{:S(2)}) copy-start(f32[3,64,72]{2,1,0:T(8,128)} %get-tuple-element.11) | copy-start | bytes 165892

commit v3 on v2

--- a/solution.py
+++ b/solution.py
@@ -32,7 +32,8 @@
 
 
 def kernel(
-    dims, x, u, sw, tw, out, ig, sg, tgrad,
+    dims, x_in, u_in, sw_in, tw_in, out, ig, sg, tgrad,
+    x, u, sw, tw, load_sem,
     wf, wi, tg, to,
     xh, uh, hid, gs, gh, ga, o_own, o_send, o_recv, i_own, i_send, i_recv,
     acc, rs_send, rs_recv, red,
@@ -72,20 +73,30 @@
     for d in range(1, n):
         pl.semaphore_signal(barrier, inc=1, device_id=peer(d)[1], device_id_type=MESH)
     pl.semaphore_signal(barrier, inc=1, device_id={"chan": oc}, device_id_type=MESH)
+    loads = [
+        pltpu.make_async_copy(src, dst, load_sem.at[k])
+        for k, (src, dst) in enumerate(((tw_in, tw), (u_in, u), (sw_in, sw), (x_in, x)))
+    ]
+    for load in loads:
+        load.start()
     acc[...] = jnp.zeros_like(acc)
 
     def widen(parts):
         zero = jnp.zeros((parts[0].shape[0], MP - M), F32)
         return jnp.concatenate([v for p in parts for v in (p.astype(F32), zero)], axis=1)
 
+    loads[0].wait()
     tcol = [widen([tw[k]]) for k in range(3)]
     tg[...] = jnp.transpose(jnp.concatenate(tcol[::-1], axis=0)).astype(BF16)
     to[...] = jnp.concatenate(tcol, axis=1).astype(BF16)
+    loads[1].wait()
     ga_inner()
+    loads[2].wait()
     wide = jnp.concatenate([widen([sw[i, j] for j in range(3)]) for i in range(3)], axis=0)
     wf[...] = jnp.transpose(wide).astype(BF16)
     for i in range(3):
         wi[i] = wide[i * C : (i + 1) * C].astype(BF16)
+    loads[3].wait()
     pl.semaphore_wait(barrier, n)
 
     def remote(src, dst, s, r, dev):
@@ -97,14 +108,14 @@
     down_dev = {"axial": jnp.minimum(a + 1, A - 1)}
     has_up, has_down = a > 0, a < A - 1
     def x_down(f):
-        return remote(x.at[f, H - 1], xh.at[0, f], xs_sem.at[0, f], xr_sem.at[0, f], down_dev)
+        return remote(x_in.at[f, H - 1], xh.at[0, f], xs_sem.at[0, f], xr_sem.at[0, f], down_dev)
 
     def x_up(f):
-        return remote(x.at[f, 0], xh.at[1, f], xs_sem.at[1, f], xr_sem.at[1, f], up_dev)
+        return remote(x_in.at[f, 0], xh.at[1, f], xs_sem.at[1, f], xr_sem.at[1, f], up_dev)
 
     order = [0, F - 1] + list(range(1, F - 1))
-    u_next = remote(u.at[F - 1], uh.at[0], us_sem.at[0], ur_sem.at[0], {"tm": next_t})
-    u_prev = remote(u.at[0], uh.at[1], us_sem.at[1], ur_sem.at[1], {"tm": prev_t})
+    u_next = remote(u_in.at[F - 1], uh.at[0], us_sem.at[0], ur_sem.at[0], {"tm": next_t})
+    u_prev = remote(u_in.at[0], uh.at[1], us_sem.at[1], ur_sem.at[1], {"tm": prev_t})
 
     @pl.when(has_down)
     def _():
@@ -320,6 +331,16 @@
 
 
 T0 = 256
+VMEM_BYTES = 24 * 1024 * 1024
+
+
+def store_kernel(*refs):
+    sems = refs[8]
+    copies = [pltpu.make_async_copy(refs[k], refs[4 + k], sems.at[k]) for k in range(4)]
+    for copy in copies:
+        copy.start()
+    for copy in copies:
+        copy.wait()
 
 
 def shards(x, sw, tw, u):
@@ -334,18 +355,24 @@
     owners = R // rp
     CS = C // 2
     vm = pl.BlockSpec(memory_space=pltpu.VMEM)
+    hbm = pl.BlockSpec(memory_space=pltpu.HBM)
     dma = pltpu.SemaphoreType.DMA
-    out, ig, sgrad, tgrad = pl.pallas_call(
+    results = pl.pallas_call(
         functools.partial(kernel, (F, H, C, W, M, MP, T, A, factor, owners, rp)),
         out_shape=(
-            jax.ShapeDtypeStruct((F, H, CS, W), BF16),
-            jax.ShapeDtypeStruct((F, H, CS, W), BF16),
-            jax.ShapeDtypeStruct((3, 3, C, M), F32),
-            jax.ShapeDtypeStruct((3, C, M), F32),
+            pltpu.VMEM((F, H, CS, W), BF16),
+            pltpu.VMEM((F, H, CS, W), BF16),
+            pltpu.VMEM((3, 3, C, M), F32),
+            pltpu.VMEM((3, C, M), F32),
         ),
-        in_specs=[vm] * 4,
+        in_specs=[hbm] * 4,
         out_specs=[vm] * 4,
         scratch_shapes=[
+            pltpu.VMEM((F, H, C, W), BF16),
+            pltpu.VMEM((F, H, C, W), BF16),
+            pltpu.VMEM((3, 3, C, M), BF16),
+            pltpu.VMEM((3, C, M), BF16),
+            dma((4,)),
             pltpu.VMEM((3 * MP, 3 * C), BF16),
             pltpu.VMEM((3, C, 3 * MP), BF16),
             pltpu.VMEM((MP, 3 * C), BF16),
@@ -371,8 +398,16 @@
             dma((F,)), dma((F,)), dma((F,)), dma((F,)),
             dma((n - 1,)), dma((n - 1,)), dma((n - 1,)), dma((n - 1,)),
         ],
-        compiler_params=pltpu.CompilerParams(collective_id=0, has_side_effects=True),
-    )(x, u, sw, jnp.transpose(tw, (0, 2, 1)))
+        compiler_params=pltpu.CompilerParams(collective_id=0, has_side_effects=True, vmem_limit_bytes=VMEM_BYTES),
+    )(*(pltpu.with_memory_space_constraint(v, pltpu.HBM) for v in (x, u, sw, jnp.transpose(tw, (0, 2, 1)))))
+    out, ig, sgrad, tgrad = pl.pallas_call(
+        store_kernel,
+        out_shape=[jax.ShapeDtypeStruct(r.shape, r.dtype) for r in results],
+        in_specs=[vm] * 4,
+        out_specs=[hbm] * 4,
+        scratch_shapes=[dma((4,))],
+        compiler_params=pltpu.CompilerParams(vmem_limit_bytes=VMEM_BYTES),
+    )(*results)
     return out, ig, sgrad, jnp.transpose(tgrad, (0, 2, 1))
 
 

time: 32.4 us -> 27.5 us (0.85)
  local copies, waits for them, and re-layouts: 4.29 us -> 0 us
  Pallas kernels: 27.2 us -> 26.7 us
    unnamed x10 -> x0, local copies, waits for them, and re-layouts: 4.29 us -> none
    pallas_call x1, Pallas kernels: 27.2 us -> 25.8 us  [shards(): pl.pallas_call(functools.partial(kernel, (F, H, C, W, M, MP, T, A, factor...]
    pallas_call x0 -> x1, Pallas kernels: none -> 0.9 us  [shards(): pl.pallas_call(store_kernel, out_shape=[jax.ShapeDtypeStruct(r.shape, r.d...]
where the time goes in v3:
time: 27.5 us; the launch traced here: 27.4 us
  Pallas kernels  26.7 us (97%)
  between operations  0.64 us (2%)
    pallas_call x1, Pallas kernels, shards(): pl.pallas_call(functools.partial(kernel, (F, H, C, W, M, MP, T, A, factor...  25.8 us
    pallas_call x1, Pallas kernels, shards(): pl.pallas_call(store_kernel, out_shape=[jax.ShapeDtypeStruct(r.shape, r.d...  0.9 us

profile of v3, /device:TPU:0, one launch (start us, length us, event | category | flops | bytes accessed | tf_op | source)
XLA Modules:
  0.0 27.4 jit_solution(6257588105351519736)
XLA Ops:
  0.6 25.8 %shard_map.75 = (bf16[6,4,32,128]{3,2,1,0:T(8,128)(2,1)S(1)}, bf16[6,4,32,128]{3,2,1,0:T(8,128)(2,1)S(1)}, f32[3,3,64,72]{3,2,1,0:T(8,128)S(1)}, f32[3,64,72]{2,1,0:T(8,128)S(1)}) custom-call(bf16[6,4,64,128]{3,2,1,0:T(8,128)(2,1)} %x_in.1, bf16[6,4,64,128]{3,2,1,0:T(8,128)(2,1)} %u_in.1, bf16[3,3,64,72]{3,2,1,0:T(8,128)(2,1)} %sw_in.1, ...), custom_call_target="tpu_custom_call" | custom-call | tf_op jit(solution)/shard_map/pallas_call | solution.py:360
  26.5 0.9 %shard_map.76 = (bf16[6,4,32,128]{3,2,1,0:T(8,128)(2,1)}, bf16[6,4,32,128]{3,2,1,0:T(8,128)(2,1)}, f32[3,3,64,72]{3,2,1,0:T(8,128)}, f32[3,64,72]{2,1,0:T(8,128)}) custom-call(bf16[6,4,32,128]{3,2,1,0:T(8,128)(2,1)S(1)} %get-tuple-element.12.refs_0_, bf16[6,4,32,128]{3,2,1,0:T(8,128)(2,1)S(1)} %get-tuple-element.13.refs_1_, ...), custom_call_target="tpu_custom_call" | custom-call | tf_op jit(solution)/shard_map/pallas_call | solution.py:403

commit v4 on v3

--- a/solution.py
+++ b/solution.py
@@ -36,13 +36,15 @@
     x, u, sw, tw, load_sem,
     wf, wi, tg, to,
     xh, uh, hid, gs, gh, ga, o_own, o_send, o_recv, i_own, i_send, i_recv,
-    acc, rs_send, rs_recv, red,
+    acc, packed, rs_send, rs_recv, red,
     xs_sem, xr_sem, us_sem, ur_sem, hs_sem, hr_sem, gs_sem, gr_sem,
     os_sem, or_sem, is_sem, ir_sem, rss_sem, rsr_sem, ags_sem, agr_sem,
 ):
     F, H, C, W, M, MP, T, A, factor, owners, rp = dims
     CS = C // 2
     n = T * A
+    FR, LW = 3 * C // 4, 4 * M - 256
+    nb = -(-FR // (8 * owners))
     t, a, ch = lax.axis_index("tm"), lax.axis_index("axial"), lax.axis_index("chan")
     oc = 1 - ch
     g = t * A + a
@@ -113,7 +115,8 @@
     def x_up(f):
         return remote(x_in.at[f, 0], xh.at[1, f], xs_sem.at[1, f], xr_sem.at[1, f], up_dev)
 
-    order = [0, F - 1] + list(range(1, F - 1))
+    inner = list(range(1, F - 1))
+    order = inner[: len(inner) // 2] + [0, F - 1] + inner[len(inner) // 2 :]
     u_next = remote(u_in.at[F - 1], uh.at[0], us_sem.at[0], ur_sem.at[0], {"tm": next_t})
     u_prev = remote(u_in.at[0], uh.at[1], us_sem.at[1], ur_sem.at[1], {"tm": prev_t})
 
@@ -140,11 +143,6 @@
         xh[1] = jnp.zeros((F, C, W), BF16)
         gh[1] = jnp.zeros((F, MP, W), BF16)
 
-    u_next.wait_recv()
-    u_prev.wait_recv()
-    for f in (0, F - 1):
-        ga[f] = mm(tg[...], u_stack(f))
-
     h_next = remote(hid.at[F], hid.at[0], hs_sem.at[0], hr_sem.at[0], {"tm": next_t})
     h_prev = remote(hid.at[1], hid.at[F + 1], hs_sem.at[1], hr_sem.at[1], {"tm": prev_t})
 
@@ -163,6 +161,11 @@
         def _():
             x_up(f).wait_recv()
 
+        if f == 0:
+            u_next.wait_recv()
+            u_prev.wait_recv()
+        if f in (0, F - 1):
+            ga[f] = mm(tg[...], u_stack(f))
         rows = [xh[0, f]] + [x[f, h] for h in range(H)] + [xh[1, f]]
         xst = lanes([jnp.concatenate(rows[h : h + 3], axis=0) for h in range(H)])
         y = mm(wf[...], xst)
@@ -197,8 +200,20 @@
         acc[:, 0 : 3 * MP] += mm_nt(xst, lanes(gsh))
         acc[:, T0 : T0 + MP] += mm_nt(u_stack(f), lanes(hs))
 
+    dense = jnp.concatenate(
+        [acc[:, j * MP : j * MP + M] for j in range(3)] + [acc[:, T0 : T0 + M]], axis=1
+    ) * factor
+    rest = dense[:, 256:]
+    folded = jnp.concatenate([rest[q * FR : (q + 1) * FR] for q in range(4)], axis=1)
+    if owners * nb * 8 > FR:
+        spare = jnp.zeros((owners * nb * 8 - FR, 128), F32)
+        folded = jnp.concatenate([folded, spare], axis=0)
     for p in range(owners):
-        rs_send[p] = (acc[p * rp : (p + 1) * rp] * factor).astype(BF16)
+        block = dense[p * rp : (p + 1) * rp]
+        tail = folded[p * nb * 8 : (p + 1) * nb * 8]
+        block = jnp.concatenate([block[:, :128], block[:, 128:256], tail], axis=0)
+        packed[p] = block
+        rs_send[p] = block.astype(BF16)
 
     def rs_copy(d):
         p, dev = peer(d)
@@ -223,11 +238,7 @@
     def i_copy(f):
         return remote(i_send.at[f], i_recv.at[f], is_sem.at[f], ir_sem.at[f], {"chan": oc})
 
-    for f in list(range(1, F - 1)) + [0, F - 1]:
-        if f == 0:
-            h_next.wait_recv()
-        if f == F - 1:
-            h_prev.wait_recv()
+    def output_frame(f):
         st = lanes([jnp.concatenate([hid[f + k, h] for k in range(3)], axis=0) for h in range(H)])
         y = mm(to2, st)
         for h in range(H):
@@ -236,13 +247,16 @@
             o_send[f, h] = y[CS:, sl].astype(BF16)
         o_copy(f).start()
 
+    for f in inner:
+        output_frame(f)
+
     def ag_copy(d):
         _, dev = peer(d)
         mine = red.at[lax.rem(g, owners)]
         return remote(mine, mine, ags_sem.at[d - 1], agr_sem.at[d - 1], dev)
 
     def reduce_piece():
-        total = acc[pl.ds(pl.multiple_of(lax.rem(g, owners) * rp, 8), rp), :] * factor
+        total = packed[lax.rem(g, owners)]
         for d in range(1, n):
             rs_copy(d).wait_recv()
             total = total + rs_recv[d - 1].astype(F32)
@@ -253,10 +267,7 @@
     wi2 = jnp.concatenate(
         [wi[i, own_rows, :] for i in range(3)] + [wi[i, far_rows, :] for i in range(3)], axis=0
     )
-    for f in range(F):
-        if f == F // 2:
-            guarded(g < owners, reduce_piece)
-
+    for f in order:
         @pl.when(has_up)
         def _():
             g_down(f).wait_recv()
@@ -284,6 +295,11 @@
             i_send[f, h] = part(3 * CS).astype(BF16)
         i_copy(f).start()
 
+    guarded(g < owners, reduce_piece)
+    h_next.wait_recv()
+    output_frame(0)
+    h_prev.wait_recv()
+    output_frame(F - 1)
     for f in range(F):
         o_copy(f).wait_recv()
         out[f] = (o_own[f] + o_recv[f].astype(F32)).astype(BF16)
@@ -299,12 +315,21 @@
             remote(dst, dst, ags_sem.at[d - 1], agr_sem.at[d - 1], peer(n - d)[1]).wait_recv()
 
         guarded(src < owners, arrive)
-    total = jnp.concatenate([red[p].astype(F32) for p in range(owners)], axis=0)
+    got = [red[p].astype(F32) for p in range(owners)]
+    tails = jnp.concatenate([v[2 * rp :] for v in got], axis=0)[:FR]
+    total = jnp.concatenate(
+        [
+            jnp.concatenate([v[:rp] for v in got], axis=0),
+            jnp.concatenate([v[rp : 2 * rp] for v in got], axis=0),
+            jnp.concatenate([tails[:, q * LW : (q + 1) * LW] for q in range(4)], axis=0),
+        ],
+        axis=1,
+    )
     for i in range(3):
         for j in range(3):
-            sg[i, j] = total[i * C : (i + 1) * C, j * MP : j * MP + M]
+            sg[i, j] = total[i * C : (i + 1) * C, j * M : (j + 1) * M]
     for k in range(3):
-        tgrad[2 - k] = total[k * C : (k + 1) * C, T0 : T0 + M]
+        tgrad[2 - k] = total[k * C : (k + 1) * C, 3 * M :]
 
     @pl.when(has_down)
     def _():
@@ -353,6 +378,7 @@
     R, L = 3 * C, T0 + 128
     rp = next(r for r in range(8, R + 1, 8) if R % r == 0 and R // r <= n)
     owners = R // rp
+    PR = 2 * rp + 8 * -(-R // (32 * owners))
     CS = C // 2
     vm = pl.BlockSpec(memory_space=pltpu.VMEM)
     hbm = pl.BlockSpec(memory_space=pltpu.HBM)
@@ -390,9 +416,10 @@
             pltpu.VMEM((F, H, CS, W), BF16),
             pltpu.VMEM((F, H, CS, W), BF16),
             pltpu.VMEM((R, L), F32),
-            pltpu.VMEM((owners, rp, L), BF16),
-            pltpu.VMEM((n - 1, rp, L), BF16),
-            pltpu.VMEM((owners, rp, L), BF16),
+            pltpu.VMEM((owners, PR, 128), F32),
+            pltpu.VMEM((owners, PR, 128), BF16),
+            pltpu.VMEM((n - 1, PR, 128), BF16),
+            pltpu.VMEM((owners, PR, 128), BF16),
             dma((2, F)), dma((2, F)), dma((2,)), dma((2,)), dma((2,)), dma((2,)),
             dma((2, F)), dma((2, F)),
             dma((F,)), dma((F,)), dma((F,)), dma((F,)),

time: 27.5 us -> 25.9 us (0.942)
  Pallas kernels: 26.7 us -> 25.1 us
    pallas_call x1, Pallas kernels: 25.8 us -> 24.2 us  [shards(): pl.pallas_call(functools.partial(kernel, (F, H, C, W, M, MP, T, A, factor...]
where the time goes in v4:
time: 25.9 us; the launch traced here: 25.7 us
  Pallas kernels  25.1 us (97%)
  between operations  0.64 us (2%)
    pallas_call x1, Pallas kernels, shards(): pl.pallas_call(functools.partial(kernel, (F, H, C, W, M, MP, T, A, factor...  24.2 us
    pallas_call x1, Pallas kernels, shards(): pl.pallas_call(store_kernel, out_shape=[jax.ShapeDtypeStruct(r.shape, r.d...  0.9 us

profile of v4, /device:TPU:0, one launch (start us, length us, event | category | flops | bytes accessed | tf_op | source)
XLA Modules:
  0.0 25.7 jit_solution(879726193046588012)
XLA Ops:
  0.6 24.2 %shard_map.75 = (bf16[6,4,32,128]{3,2,1,0:T(8,128)(2,1)S(1)}, bf16[6,4,32,128]{3,2,1,0:T(8,128)(2,1)S(1)}, f32[3,3,64,72]{3,2,1,0:T(8,128)S(1)}, f32[3,64,72]{2,1,0:T(8,128)S(1)}) custom-call(bf16[6,4,64,128]{3,2,1,0:T(8,128)(2,1)} %x_in.1, bf16[6,4,64,128]{3,2,1,0:T(8,128)(2,1)} %u_in.1, bf16[3,3,64,72]{3,2,1,0:T(8,128)(2,1)} %sw_in.1, ...), custom_call_target="tpu_custom_call" | custom-call | tf_op jit(solution)/shard_map/pallas_call | solution.py:386
  24.8 0.9 %shard_map.76 = (bf16[6,4,32,128]{3,2,1,0:T(8,128)(2,1)}, bf16[6,4,32,128]{3,2,1,0:T(8,128)(2,1)}, f32[3,3,64,72]{3,2,1,0:T(8,128)}, f32[3,64,72]{2,1,0:T(8,128)}) custom-call(bf16[6,4,32,128]{3,2,1,0:T(8,128)(2,1)S(1)} %get-tuple-element.12.refs_0_, bf16[6,4,32,128]{3,2,1,0:T(8,128)(2,1)S(1)} %get-tuple-element.13.refs_1_, ...), custom_call_target="tpu_custom_call" | custom-call | tf_op jit(solution)/shard_map/pallas_call | solution.py:430
